TPU v7x, 256 devices: a whole 4x4x8 slice. The times are simulated.
256 devices in a mesh: ctx: 64 (over y, z_lo, x, core), tp: 4 (over z_hi).
Axes of the slice: x: 4, y: 4, z: 8 (z_hi: 4, z_lo: 2; z = z_hi * 2 + z_lo), core: 2. Of those that a mesh axis runs over, the one named last changes fastest.
Arguments:
- queries: bfloat16 [16384, 2048], P('ctx', 'tp'), may hold values from -8 to 8
- span_keys: bfloat16 [16384, 1024], P('ctx', 'tp'), may hold values from -6 to 6
- span_values: bfloat16 [16384, 1024], P('ctx', 'tp'), may hold values from -6 to 6
- cache_keys: bfloat16 [8192, 1024], P('ctx', 'tp'), may hold values from -8 to 8
- cache_values: bfloat16 [8192, 1024], P('ctx', 'tp'), may hold values from -6 to 6
- out_weight: bfloat16 [2048, 3840], P('tp'), may hold values from -0.125 to 0.125
- offsets: int32 [64], replicated, may hold values from 0 to 16128, as said below
- earlier_block_slot: int32 [128], replicated, may hold values from 0 to 127, each once
- prior_block_count: int32 [1], replicated, may hold values from 32 to 127
Outputs:
- projected: bfloat16 [16384, 3840], P('ctx', 'tp')
Inputs may be any that keep to these rules, and one draw needn't show every extreme that they name: `offsets`: a permutation of the multiples of 256 below 16384. Block b of the earlier prompt lies in slot earlier_block_slot[b]; slot s is held by index s // 2 of ctx; only blocks below prior_block_count[0] are valid.
All inputs are finite; a program needn't handle non-finite values.
Results may differ from a plain program's by a relative error of at most 0.012.
Values may be sent and summed in bfloat16 or wider, within the bound.
No kernel may reach another device: no remote copies, remote signals or barrier semaphores. Data moves between devices by JAX's collectives and lax.ppermute only.
A program may use at most 192 MiB of HBM per device.

v0:
```python
import jax
import jax.numpy as jnp
from jax import lax
from jax.sharding import PartitionSpec as P

E = 256
BLK = 64


def per_device(
    queries,
    span_keys,
    span_values,
    cache_keys,
    cache_values,
    out_weight,
    offsets,
    earlier_block_slot,
    prior_block_count,
):
    local_tokens = queries.shape[0]
    kv_local = span_keys.shape[1] // E
    q_local = queries.shape[1] // E
    query_group_width = q_local // kv_local
    query_rows = query_group_width * local_tokens
    shard_count = lax.axis_size("ctx")
    my_shard = lax.axis_index("ctx")
    shard_ids = jnp.arange(shard_count, dtype=jnp.int32)
    my_offset = jnp.sum(jnp.where(shard_ids == my_shard, offsets, 0))
    query_pos = my_offset + jnp.arange(local_tokens, dtype=jnp.int32)
    row_pos = jnp.tile(query_pos, query_group_width)
    slot_count = earlier_block_slot.shape[0]
    slot_ids = jnp.arange(slot_count, dtype=jnp.int32)
    slot_owner_block = jnp.sum(
        jnp.where(earlier_block_slot[None, :] == slot_ids[:, None], slot_ids[None, :], 0), axis=1
    )
    live_slot = slot_owner_block < prior_block_count[0]
    grouped = (
        queries.reshape(local_tokens, kv_local, query_group_width, E)
        .transpose(1, 2, 0, 3)
        .reshape(kv_local, query_rows, E)
    )
    scale = E ** (-0.5)

    def absorb(carry, key_rows, value_rows, allowed):
        largest, total, summed = carry
        new_largest, new_total, new_summed = ([], [], [])
        scores = (
            jnp.einsum("re,ne->rn", grouped[0], key_rows, preferred_element_type=jnp.float32)
            * scale
        )
        scores = jnp.where(allowed, scores, -1e30)
        peak = jnp.maximum(largest[0], jnp.max(scores, axis=1))
        weights = jnp.where(allowed, jnp.exp(scores - peak[:, None]), 0.0)
        factor = jnp.exp(largest[0] - peak)
        new_largest.append(peak)
        new_total.append(total[0] * factor + jnp.sum(weights, axis=1))
        update = jnp.dot(
            weights.astype(jnp.bfloat16), value_rows, preferred_element_type=jnp.float32
        )
        new_summed.append(summed[0] * factor[:, None] + update)
        return (jnp.stack(new_largest), jnp.stack(new_total), jnp.stack(new_summed))

    def guarded(carry, key_rows, value_rows, allowed):
        return absorb(carry, key_rows, value_rows, allowed)

    initial = (
        jnp.full((kv_local, query_rows), -1e30, jnp.float32),
        jnp.zeros((kv_local, query_rows), jnp.float32),
        jnp.zeros((kv_local, query_rows, E), jnp.float32),
    )
    key_rows = lax.all_gather(cache_keys, "ctx", axis=0, tiled=True)
    value_rows = lax.all_gather(cache_values, "ctx", axis=0, tiled=True)
    row_count = key_rows.shape[0]
    slot_number = jnp.arange(row_count, dtype=jnp.int32) // BLK
    allowed = jnp.broadcast_to(
        jnp.any((slot_number[:, None] == slot_ids[None, :]) & live_slot[None, :], axis=1)[None, :],
        (query_rows, row_count),
    )
    state = guarded(initial, key_rows, value_rows, allowed)
    key_rows = lax.all_gather(span_keys, "ctx", axis=0, tiled=True)
    value_rows = lax.all_gather(span_values, "ctx", axis=0, tiled=True)
    row_count = key_rows.shape[0]
    global_row = jnp.arange(row_count, dtype=jnp.int32)
    key_pos = (
        jnp.sum(
            jnp.where(
                (global_row // local_tokens)[:, None] == shard_ids[None, :], offsets[None, :], 0
            ),
            axis=1,
        )
        + global_row % local_tokens
    )
    allowed = key_pos[None, :] <= row_pos[:, None]
    state = guarded(state, key_rows, value_rows, allowed)
    largest, total, summed = state
    attended = summed / total[:, :, None]
    attended = (
        attended.reshape(kv_local, query_group_width, local_tokens, E)
        .transpose(2, 0, 1, 3)
        .reshape(local_tokens, q_local * E)
        .astype(jnp.bfloat16)
    )
    partial_out = jnp.dot(attended, out_weight, preferred_element_type=jnp.float32)
    return lax.psum_scatter(partial_out.astype(jnp.bfloat16), "tp", scatter_dimension=1, tiled=True)


def solution(mesh):
    placed = (
        P("ctx", "tp"),
        P("ctx", "tp"),
        P("ctx", "tp"),
        P("ctx", "tp"),
        P("ctx", "tp"),
        P("tp", None),
        P(),
        P(),
        P(),
    )
    return jax.shard_map(
        per_device, mesh=mesh, in_specs=placed, out_specs=P("ctx", "tp"), check_vma=False
    )
```

profile of v0, /device:TPU:1, one launch (start us, length us, event | category | flops | bytes accessed | tf_op | source)
XLA Modules:
  0.0 531.4 jit_solution(16656678070115511567)
XLA Ops:
  6.5 0.0 all-gather.5.cloned.1.call-start
  6.5 0.7 all-gather.5.cloned.1.call-update
  7.3 0.0 all-gather.9.cloned.1.call-start
  7.3 0.7 all-gather.9.cloned.1.call-update
  8.0 0.0 all-gather.7.cloned.1.call-start
  8.1 0.7 all-gather.7.cloned.1.call-update
  8.7 0.0 all-gather.11.cloned.1.call-start
  8.8 0.5 all-gather.11.cloned.1.call-update
  9.3 0.0 reduce-scatter.2.cloned.1.call-start
  9.4 1.3 fusion.39
  10.7 0.6 iota_add_fusion
  11.3 1.1 copy.14
  12.4 0.1 copy.15
  13.2 0.8 select_reduce_fusion.1
  14.0 2.6 fusion.12
  16.6 1.4 select_reduce_fusion
  18.0 103.0 %all-gather.5.cloned.1.call-done = bf16[8192,256]{1,0:T(8,128)(2,1)} async-done(((bf16[128,256]{1,0:T(8,128)(2,1)}), bf16[8192,256]{1,0:T(8,128)(2,1)}) %all-gather.5.cloned.1.call-update) | async-done | bytes 4194320 | tf_op jit(solution)/shard_map/all_gather | solution.py:72
  121.0 9.4 %fusion.5 = (f32[512]{0:T(512)S(1)}, f32[512,8192]{1,0:T(8,128)}) fusion(pred[8192]{0:T(1024)(128)(4,1)S(1)} %fusion.12, bf16[512,256]{1,0:T(8,128)(2,1)S(1)} %bitcast.23, bf16[8192,256]{1,0:T(8,128)(2,1)} %all-gather.5.cloned.1.call-done), kind=kOutput, calls=%fused_computation.8 | convolution fusion | flops 2160066048 | bytes 21243904 | tf_op jit(solution)/shard_map/re,ne->rn/dot_general | solution.py:49
  130.4 104.0 %all-gather.9.cloned.1.call-done = bf16[16384,256]{1,0:T(8,128)(2,1)} async-done(((bf16[256,256]{1,0:T(8,128)(2,1)}), bf16[16384,256]{1,0:T(8,128)(2,1)}) %all-gather.9.cloned.1.call-update) | async-done | bytes 8388624 | tf_op jit(solution)/shard_map/all_gather | solution.py:81
  234.4 17.2 %fusion = (f32[512]{0:T(512)S(1)}, f32[512,16384]{1,0:T(8,128)}) fusion(s32[16384]{0:T(1024)S(1)} %fusion.34, s32[512]{0:T(512)S(1)} %bitcast.26, bf16[512,256]{1,0:T(8,128)(2,1)S(1)} %bitcast.24, bf16[16384,256]{1,0:T(8,128)(2,1)} %all-gather.9.cloned.1.call-done), kind=kOutput, calls=%fused_computation.2 | convolution fusion | flops 4328521216 | bytes 42274816 | tf_op jit(solution)/shard_map/re,ne->rn/dot_general | solution.py:49
  251.6 8.6 %fusion.6 = f32[512]{0:T(512)S(1)} fusion(f32[512,8192]{1,0:T(8,128)} %get-tuple-element.11, f32[512]{0:T(512)S(1)} %get-tuple-element.9, pred[8192]{0:T(1024)(128)(4,1)S(1)} %fusion.12), kind=kLoop, calls=%fused_computation.9 | loop fusion | flops 20971008 | bytes 16789504 | tf_op jit(solution)/shard_map/reduce_sum | solution.py:57
  260.2 15.9 %fusion.1 = f32[512]{0:T(512)S(1)} fusion(f32[512,16384]{1,0:T(8,128)} %get-tuple-element.13, f32[512]{0:T(512)S(1)} %get-tuple-element.8, s32[16384]{0:T(1024)S(1)} %fusion.34, s32[512]{0:T(512)S(1)} %bitcast.27), kind=kLoop, calls=%fused_computation.3 | loop fusion | flops 50331136 | bytes 33626112 | tf_op jit(solution)/shard_map/reduce_sum | solution.py:57
  276.1 66.8 %all-gather.7.cloned.1.call-done = bf16[8192,256]{1,0:T(8,128)(2,1)} async-done(((bf16[128,256]{1,0:T(8,128)(2,1)}), bf16[8192,256]{1,0:T(8,128)(2,1)}) %all-gather.7.cloned.1.call-update) | async-done | bytes 4194320 | tf_op jit(solution)/shard_map/all_gather | solution.py:73
  342.9 8.8 %fusion.19 = f32[512,256]{1,0:T(8,128)S(1)} fusion(bf16[8192,256]{1,0:T(8,128)(2,1)} %all-gather.7.cloned.1.call-done, f32[512,8192]{1,0:T(8,128)} %get-tuple-element.11, f32[512]{0:T(512)S(1)} %get-tuple-element.9, pred[8192]{0:T(1024)(128)(4,1)S(1)} %fusion.12, f32[512]{0:T(512)S(1)} %get-tuple-element.6, f32[512]{0:T(512)S(1)} %get-tuple-element.7), kind=kOutput, calls=%fused_computation.21 | convolution fusion | flops 2168717312 | bytes 21510144 | tf_op jit(solution)/shard_map/dot_general | solution.py:58
  351.7 104.4 %all-gather.11.cloned.1.call-done = bf16[16384,256]{1,0:T(8,128)(2,1)} async-done(((bf16[256,256]{1,0:T(8,128)(2,1)}), bf16[16384,256]{1,0:T(8,128)(2,1)}) %all-gather.11.cloned.1.call-update) | async-done | bytes 8388624 | tf_op jit(solution)/shard_map/all_gather | solution.py:82
  456.1 16.8 %fusion.25 = bf16[512,256]{1,0:T(8,128)(2,1)S(1)} fusion(f32[512,256]{1,0:T(8,128)S(1)} %fusion.19, bf16[16384,256]{1,0:T(8,128)(2,1)} %all-gather.11.cloned.1.call-done, f32[512,16384]{1,0:T(8,128)} %get-tuple-element.13, f32[512]{0:T(512)S(1)} %get-tuple-element.8, s32[16384]{0:T(1024)S(1)} %fusion.34, s32[512]{0:T(512)S(1)} %bitcast.28, ...), kind=kOutput, calls=%fused_computation.23 | convolution fusion | flops 4345692160 | bytes 42801152 | tf_op jit(solution)/shard_map/dot_general | solution.py:58
  472.9 0.1 copy.16
  473.0 5.0 convolution_convert_fusion
  478.1 0.0 reduce-scatter.2.cloned.1.call-update
  478.1 46.8 %reduce-scatter.2.cloned.1.call-done = bf16[256,960]{0,1:T(8,128)(2,1)} async-done(((bf16[256,3840]{0,1:T(8,128)(2,1)}), bf16[256,960]{0,1:T(8,128)(2,1)}) %reduce-scatter.2.cloned.1.call-update) | async-done | bytes 491536 | tf_op jit(solution)/shard_map/reduce_scatter | solution.py:105
  (8 shorter events, 0.1 us)
Async XLA Ops:
  6.5 114.5 %all-gather.5.cloned.1.call-start = ((), (), s32[]{:S(2)}) async-start(), calls=%async_computation.1 | async-start | bytes 4259840 | tf_op jit(solution)/shard_map/all_gather | solution.py:72
  7.3 227.1 %all-gather.9.cloned.1.call-start = ((), (), s32[]{:S(2)}) async-start(), calls=%async_computation.3 | async-start | bytes 8519680 | tf_op jit(solution)/shard_map/all_gather | solution.py:81
  8.0 334.9 %all-gather.7.cloned.1.call-start = ((), (), s32[]{:S(2)}) async-start(), calls=%async_computation.2 | async-start | bytes 4259840 | tf_op jit(solution)/shard_map/all_gather | solution.py:73
  8.7 447.4 %all-gather.11.cloned.1.call-start = ((), (), s32[]{:S(2)}) async-start(), calls=%async_computation.4 | async-start | bytes 8519680 | tf_op jit(solution)/shard_map/all_gather | solution.py:82
  9.3 515.6 %reduce-scatter.2.cloned.1.call-start = ((), (), s32[]{:S(2)}) async-start(), calls=%async_computation.5 | async-start | bytes 2457600 | tf_op jit(solution)/shard_map/reduce_scatter | solution.py:105
Sparse Core Ops, SparseCore 0:
  9.2 111.7 all-gather.4
  122.9 111.4 all-gather.8
  236.3 106.5 all-gather.6
  344.6 111.4 all-gather.10
  478.2 46.6 reduce-scatter.1
where the time goes:
time: 532 us; the launch traced here: 531 us
  waiting for transfers between devices  428 us (80%)
  matrix products  57.2 us (11%)
  other arithmetic  31.2 us (6%)
  between operations  13.9 us (3%)
    all_gather x1, waiting for transfers between devices, per_device(): value_rows = lax.all_gather(span_values, 'ctx', axis=0, tiled=True)  104 us
    all_gather x1, waiting for transfers between devices, per_device(): key_rows = lax.all_gather(span_keys, 'ctx', axis=0, tiled=True)  104 us
    all_gather x1, waiting for transfers between devices, per_device(): key_rows = lax.all_gather(cache_keys, 'ctx', axis=0, tiled=True)  103 us
    all_gather x1, waiting for transfers between devices, per_device(): value_rows = lax.all_gather(cache_values, 'ctx', axis=0, tiled=True)  66.8 us
    reduce_scatter x1, waiting for transfers between devices, per_device(): lax.psum_scatter(partial_out.astype(jnp.bfloat16), 'tp', scatter_dimensio...  46.8 us
    dot_general x2, matrix products, absorb(): jnp.einsum('re,ne->rn', grouped[0], key_rows, preferred_element_type=jnp....  26.6 us
    dot_general x2, matrix products, absorb(): jnp.dot(weights.astype(jnp.bfloat16), value_rows, preferred_element_type=...  25.6 us
    reduce_sum x2, other arithmetic, absorb(): new_total.append(total[0] * factor + jnp.sum(weights, axis=1))  24.5 us
  transfers between devices with their start and end apart: 5, of which 5 were waited for; matrix products, arithmetic and copies ran while one was open for 13% of the time, Pallas kernels for 0%

commit v1 on v0

--- a/solution.py
+++ b/solution.py
@@ -5,6 +5,16 @@
 
 E = 256
 BLK = 64
+
+
+def recover_spans(arr, matrix, lane_axis):
+    return jnp.split(
+        jax.lax.all_gather(
+            jnp.concatenate([arr, matrix], 1), axis_name=lane_axis, axis=0, tiled=True
+        ),
+        [arr.shape[1]],
+        1,
+    )
 
 
 def per_device(
@@ -69,8 +79,7 @@
         jnp.zeros((kv_local, query_rows), jnp.float32),
         jnp.zeros((kv_local, query_rows, E), jnp.float32),
     )
-    key_rows = lax.all_gather(cache_keys, "ctx", axis=0, tiled=True)
-    value_rows = lax.all_gather(cache_values, "ctx", axis=0, tiled=True)
+    key_rows, value_rows = recover_spans(cache_keys, cache_values, "ctx")
     row_count = key_rows.shape[0]
     slot_number = jnp.arange(row_count, dtype=jnp.int32) // BLK
     allowed = jnp.broadcast_to(

time: 532 us -> 429 us (0.81)
  waiting for transfers between devices: 428 us -> 324 us
    all_gather x2 -> x1, waiting for transfers between devices: 170 us -> 108 us  [recover_spans(): jax.lax.all_gather(jnp.concatenate([arr, matrix], 1), axis_name=lane_axis...]
    all_gather x1, waiting for transfers between devices: 104 us -> 63.4 us  [per_device(): value_rows = lax.all_gather(span_values, 'ctx', axis=0, tiled=True)]
  transfers between devices with their start and end apart: 5 -> 4, of which waited for: 5 -> 4; matrix products, arithmetic and copies ran while one was open for 13% -> 16% of each run, Pallas kernels for 0% -> 0%
where the time goes in v1:
time: 429 us
  waiting for transfers between devices  324 us (76%)
  matrix products  53.9 us (13%)
  other arithmetic  35.4 us (8%)
  between operations  14 us (3%)
    all_gather x1, waiting for transfers between devices, recover_spans(): jax.lax.all_gather(jnp.concatenate([arr, matrix], 1), axis_name=lane_axis...  108 us
    all_gather x1, waiting for transfers between devices, per_device(): key_rows = lax.all_gather(span_keys, 'ctx', axis=0, tiled=True)  104 us
    all_gather x1, waiting for transfers between devices, per_device(): value_rows = lax.all_gather(span_values, 'ctx', axis=0, tiled=True)  63.4 us
    reduce_scatter x1, waiting for transfers between devices, per_device(): lax.psum_scatter(partial_out.astype(jnp.bfloat16), 'tp', scatter_dimensio...  46.8 us
    reduce_sum x2, other arithmetic, absorb(): new_total.append(total[0] * factor + jnp.sum(weights, axis=1))  27.1 us
    dot_general x2, matrix products, absorb(): jnp.einsum('re,ne->rn', grouped[0], key_rows, preferred_element_type=jnp....  26.5 us
    dot_general x2, matrix products, absorb(): jnp.dot(weights.astype(jnp.bfloat16), value_rows, preferred_element_type=...  22.3 us
  transfers between devices with their start and end apart: 4, of which 4 were waited for; matrix products, arithmetic and copies ran while one was open for 16% of the time, Pallas kernels for 0%

profile of v1, /device:TPU:1, one launch (start us, length us, event | category | flops | bytes accessed | tf_op | source)
XLA Modules:
  0.0 428.6 jit_solution(16611576830803351531)
XLA Ops:
  6.5 0.0 all-gather.4.cloned.1.call-start
  6.5 1.5 pad_maximum_fusion
  8.1 0.0 all-gather.4.cloned.1.call-update
  8.1 0.0 all-gather.6.cloned.1.call-start
  8.1 0.7 all-gather.6.cloned.1.call-update
  8.8 0.0 all-gather.8.cloned.1.call-start
  8.9 0.7 all-gather.8.cloned.1.call-update
  9.6 0.0 reduce-scatter.2.cloned.1.call-start
  9.6 1.3 fusion.46
  11.0 0.6 iota_add_fusion
  11.6 1.1 copy.14
  12.7 0.1 copy.15
  13.5 0.8 select_reduce_fusion.1
  14.3 2.6 fusion.15
  16.9 1.4 select_reduce_fusion
  18.3 107.9 %all-gather.4.cloned.1.call-done = bf16[8192,512]{1,0:T(8,128)(2,1)} async-done(((bf16[128,512]{1,0:T(8,128)(2,1)}), bf16[8192,512]{1,0:T(8,128)(2,1)}) %all-gather.4.cloned.1.call-update) | async-done | bytes 8388624 | tf_op jit(solution)/shard_map/all_gather | solution.py:12
  126.2 9.2 %fusion.5 = (f32[512]{0:T(512)S(1)}, f32[8192,512]{1,0:T(8,128)}) fusion(pred[8192]{0:T(1024)(128)(4,1)S(1)} %fusion.15, bf16[512,256]{1,0:T(8,128)(2,1)S(1)} %bitcast.23, bf16[8192,512]{1,0:T(8,128)(2,1)} %all-gather.4.cloned.1.call-done), kind=kOutput, calls=%fused_computation.8 | convolution fusion | flops 2160066048 | bytes 21243904 | tf_op jit(solution)/shard_map/re,ne->rn/dot_general | solution.py:59
  135.4 104.4 %all-gather.6.cloned.1.call-done = bf16[16384,256]{1,0:T(8,128)(2,1)} async-done(((bf16[256,256]{1,0:T(8,128)(2,1)}), bf16[16384,256]{1,0:T(8,128)(2,1)}) %all-gather.6.cloned.1.call-update) | async-done | bytes 8388624 | tf_op jit(solution)/shard_map/all_gather | solution.py:90
  239.8 17.3 %fusion = (f32[512]{0:T(512)S(1)}, f32[512,16384]{1,0:T(8,128)}) fusion(s32[16384]{0:T(1024)S(1)} %fusion.41, s32[512]{0:T(512)S(1)} %bitcast.26, bf16[512,256]{1,0:T(8,128)(2,1)S(1)} %bitcast.24, bf16[16384,256]{1,0:T(8,128)(2,1)} %all-gather.6.cloned.1.call-done), kind=kOutput, calls=%fused_computation.2 | convolution fusion | flops 4328521216 | bytes 42274816 | tf_op jit(solution)/shard_map/re,ne->rn/dot_general | solution.py:59
  257.1 0.0 slice-start
  257.1 0.0 slice-start.1
  257.1 0.0 slice-start.4
  257.1 9.6 %fusion.6 = f32[512]{0:T(512)S(1)} fusion(f32[8192,512]{1,0:T(8,128)} %get-tuple-element.11, f32[512]{0:T(512)S(1)} %get-tuple-element.9, pred[8192]{0:T(1024)(128)(4,1)S(1)} %fusion.15), kind=kLoop, calls=%fused_computation.9 | loop fusion | flops 20971008 | bytes 16789504 | tf_op jit(solution)/shard_map/reduce_sum | solution.py:67
  266.8 0.0 slice-start.2
  266.8 0.0 slice-start.3
  266.8 0.0 slice-start.5
  266.8 17.5 %fusion.1 = f32[512]{0:T(512)S(1)} fusion(f32[512,16384]{1,0:T(8,128)} %get-tuple-element.13, f32[512]{0:T(512)S(1)} %get-tuple-element.8, s32[16384]{0:T(1024)S(1)} %fusion.41, s32[512]{0:T(512)S(1)} %bitcast.27), kind=kLoop, calls=%fused_computation.3 | loop fusion | flops 50331136 | bytes 33626112 | tf_op jit(solution)/shard_map/reduce_sum | solution.py:67
  284.3 0.0 slice-done
  284.4 0.0 slice-done.1
  284.4 0.0 slice-done.4
  284.4 0.0 slice-done.2
  284.4 0.0 slice-done.3
  284.4 0.0 slice-done.5
  284.4 5.5 %fusion.24 = f32[512,256]{1,0:T(8,128)S(1)} fusion(bf16[8192,512]{1,0:T(8,128)(2,1)S(1)} %bitcast.30, f32[8192,512]{1,0:T(8,128)S(1)} %bitcast.20, f32[512]{0:T(512)S(1)} %get-tuple-element.9, pred[8192]{0:T(1024)(128)(4,1)S(1)} %fusion.15, f32[512]{0:T(512)S(1)} %get-tuple-element.6, f32[512]{0:T(512)S(1)} %get-tuple-element.7), kind=kOutput, calls=%fused_computation.24 | convolution fusion | flops 2168717312 | bytes 21510144 | tf_op jit(solution)/shard_map/dot_general | solution.py:68
  290.0 63.4 %all-gather.8.cloned.1.call-done = bf16[16384,256]{1,0:T(8,128)(2,1)} async-done(((bf16[256,256]{1,0:T(8,128)(2,1)}), bf16[16384,256]{1,0:T(8,128)(2,1)}) %all-gather.8.cloned.1.call-update) | async-done | bytes 8388624 | tf_op jit(solution)/shard_map/all_gather | solution.py:91
  353.4 16.8 %fusion.32 = bf16[512,256]{1,0:T(8,128)(2,1)S(1)} fusion(f32[512,256]{1,0:T(8,128)S(1)} %fusion.24, bf16[16384,256]{1,0:T(8,128)(2,1)} %all-gather.8.cloned.1.call-done, f32[512,16384]{1,0:T(8,128)} %get-tuple-element.13, f32[512]{0:T(512)S(1)} %get-tuple-element.8, s32[16384]{0:T(1024)S(1)} %fusion.41, s32[512]{0:T(512)S(1)} %bitcast.28, ...), kind=kOutput, calls=%fused_computation.26 | convolution fusion | flops 4345692160 | bytes 42801152 | tf_op jit(solution)/shard_map/dot_general | solution.py:68
  370.1 0.1 copy.16
  370.3 5.0 %convolution_convert_fusion = bf16[256,3840]{0,1:T(8,128)(2,1)} fusion(bf16[256,512]{0,1:T(8,128)(2,1)S(1)} %bitcast.21, bf16[512,3840]{1,0:T(8,128)(2,1)} %param.14), kind=kOutput, calls=%fused_computation.13 | convolution fusion | flops 1007616000 | bytes 6160384 | tf_op jit(solution)/shard_map/dot_general | solution.py:113
  375.3 0.0 reduce-scatter.2.cloned.1.call-update
  375.3 46.8 %reduce-scatter.2.cloned.1.call-done = bf16[256,960]{0,1:T(8,128)(2,1)} async-done(((bf16[256,3840]{0,1:T(8,128)(2,1)}), bf16[256,960]{0,1:T(8,128)(2,1)}) %reduce-scatter.2.cloned.1.call-update) | async-done | bytes 491536 | tf_op jit(solution)/shard_map/reduce_scatter | solution.py:114
  (10 shorter events, 0.1 us)
Async XLA Ops:
  6.5 119.6 %all-gather.4.cloned.1.call-start = ((), (), s32[]{:S(2)}) async-start(), calls=%async_computation.1 | async-start | bytes 8519680 | tf_op jit(solution)/shard_map/all_gather | solution.py:12
  8.1 231.7 %all-gather.6.cloned.1.call-start = ((), (), s32[]{:S(2)}) async-start(), calls=%async_computation.2 | async-start | bytes 8519680 | tf_op jit(solution)/shard_map/all_gather | solution.py:90
  8.8 344.5 %all-gather.8.cloned.1.call-start = ((), (), s32[]{:S(2)}) async-start(), calls=%async_computation.3 | async-start | bytes 8519680 | tf_op jit(solution)/shard_map/all_gather | solution.py:91
  9.6 412.5 %reduce-scatter.2.cloned.1.call-start = ((), (), s32[]{:S(2)}) async-start(), calls=%async_computation.4 | async-start | bytes 2457600 | tf_op jit(solution)/shard_map/reduce_scatter | solution.py:114
  257.1 27.2 %slice-start = ((s8[16777216]{0:T(1024)(128)(4,1)}), s8[4194304]{0:T(1024)(128)(4,1)S(1)}, s32[]{:S(2)}) async-start(s8[16777216]{0:T(1024)(128)(4,1)} %bitcast.19), calls=%async_computation.5 | async-start | bytes 8388608
  257.1 27.2 %slice-start.1 = ((s8[16777216]{0:T(1024)(128)(4,1)}), s8[4194304]{0:T(1024)(128)(4,1)S(1)}, s32[]{:S(2)}) async-start(s8[16777216]{0:T(1024)(128)(4,1)} %bitcast.19), calls=%async_computation.6 | async-start | bytes 8388608
  257.1 27.2 %slice-start.4 = ((s8[8388608]{0:T(1024)(128)(4,1)}), s8[4194304]{0:T(1024)(128)(4,1)S(1)}, s32[]{:S(2)}) async-start(s8[8388608]{0:T(1024)(128)(4,1)} %bitcast.29), calls=%async_computation.9 | async-start | bytes 8388608
  266.8 17.6 %slice-start.2 = ((s8[16777216]{0:T(1024)(128)(4,1)}), s8[4194304]{0:T(1024)(128)(4,1)S(1)}, s32[]{:S(2)}) async-start(s8[16777216]{0:T(1024)(128)(4,1)} %bitcast.19), calls=%async_computation.7 | async-start | bytes 8388608
  266.8 17.6 %slice-start.3 = ((s8[16777216]{0:T(1024)(128)(4,1)}), s8[4194304]{0:T(1024)(128)(4,1)S(1)}, s32[]{:S(2)}) async-start(s8[16777216]{0:T(1024)(128)(4,1)} %bitcast.19), calls=%async_computation.8 | async-start | bytes 8388608
  266.8 17.6 %slice-start.5 = ((s8[8388608]{0:T(1024)(128)(4,1)}), s8[4194304]{0:T(1024)(128)(4,1)S(1)}, s32[]{:S(2)}) async-start(s8[8388608]{0:T(1024)(128)(4,1)} %bitcast.29), calls=%async_computation.10 | async-start | bytes 8388608
Sparse Core Ops, SparseCore 0:
  9.2 116.9 all-gather.3
  128.0 111.6 all-gather.5
  241.6 111.6 all-gather.7
  375.4 46.6 reduce-scatter.1
